TPU v7x, 32 devices: a whole 2x2x4 slice. The times are simulated.
32 devices in a mesh: expert: 4 (over z), dp: 8 (over y, x, core).
Axes of the slice: x: 2, y: 2, z: 4, core: 2. Of those that a mesh axis runs over, the one named last changes fastest.
Arguments:
- grad_out: bfloat16 [4096, 2048], P(('expert', 'dp')), may hold values from -1.59375 to 1.59375
- slot_token: int32 [32, 8, 8], P(('expert', 'dp')), may hold values from 0 to 127, as said below
- hidden: bfloat16 [2048, 768], P(('expert', 'dp')), may hold values from -6 to 6
- slot_weight: float32 [32, 64], P(('expert', 'dp')), may hold values from 0.05 to 0.5
- counts: int32 [32, 8], P(('expert', 'dp')), may hold values from 0 to 8, as said below
- master_weight: bfloat16 [8, 768, 2048], P('expert', 'dp')
- moment1: bfloat16 [8, 768, 2048], P('expert', 'dp')
- moment2: bfloat16 [8, 768, 2048], P('expert', 'dp'), may hold values from 0.099609375 to 2
Outputs:
- new_weight: bfloat16 [8, 768, 2048], P('expert', 'dp')
Inputs may be any that keep to these rules, and one draw needn't show every extreme that they name: `slot_token`: within one device's block for one expert, the 8 slots name different tokens. `counts`: in every draw some expert has 8 live slots from every device.
All inputs are finite; a program needn't handle non-finite values.
Results may differ from a plain program's by a relative error of at most 0.0055.
Values may be sent and summed in bfloat16 or wider, within the bound.
A program may use at most 64 MiB of HBM per device.

v0:
```python
import jax
import jax.numpy as jnp
from jax import lax
from jax.sharding import PartitionSpec as P

learn_rate = 0.3
decay_rate = 0.01
adam_eps = 1e-06
norm_eps = 1e-06
bias_one = 1.0 - 0.9**10
bias_two = 1.0 - 0.999**10


def local(grad_out, slot_token, hidden, slot_weight, counts, master_weight, moment1, moment2):
    n_expert = lax.axis_size("expert")
    experts_here = master_weight.shape[0]
    capacity = slot_token.shape[2]
    width = grad_out.shape[1]
    depth = hidden.shape[1]
    weight = master_weight.astype(jnp.float32)
    first = moment1.astype(jnp.float32)
    second = moment2.astype(jnp.float32)
    weight_sq = jnp.sum(weight * weight, axis=(1, 2))
    weight_total = lax.psum(weight_sq, "dp")
    picked = jnp.take(grad_out, slot_token.reshape(-1), axis=0).reshape(
        n_expert, experts_here * capacity, width
    )
    arrived = lax.all_to_all(picked, "expert", split_axis=0, concat_axis=0, tiled=True)
    arrived = arrived.reshape(n_expert, experts_here, capacity, width)
    slot_ids = lax.broadcasted_iota(jnp.int32, (n_expert, experts_here, capacity), 2)
    is_live = slot_ids < counts.reshape(n_expert, experts_here)[:, :, None]
    mixing = jnp.where(is_live, slot_weight.reshape(n_expert, experts_here, capacity), 0.0).astype(
        jnp.bfloat16
    )
    scaled = (mixing.astype(jnp.float32)[..., None] * arrived.astype(jnp.float32)).astype(
        jnp.bfloat16
    )
    saved = hidden.reshape(n_expert, experts_here, capacity, depth)
    shares = []
    for j in range(experts_here):
        saved_rows = saved[:, j].reshape(-1, depth)
        scaled_rows = scaled[:, j].reshape(-1, width)
        term = jnp.dot(saved_rows.T, scaled_rows, preferred_element_type=jnp.float32)
        shares.append(
            lax.psum_scatter(
                term.astype(jnp.bfloat16).astype(jnp.float32).astype(jnp.bfloat16),
                "dp",
                scatter_dimension=0,
                tiled=True,
            ).astype(jnp.float32)
        )
    gradient = jnp.stack(shares)
    first_new = 0.9 * first + 0.1 * gradient
    second_new = 0.999 * second + 0.001 * gradient * gradient
    update = (
        first_new / bias_one / (jnp.sqrt(second_new / bias_two) + adam_eps) + decay_rate * weight
    )
    update_sq = jnp.sum(update * update, axis=(1, 2))
    update_total = lax.psum(update_sq, "dp")
    trust_ratio = jnp.sqrt(weight_total) / (jnp.sqrt(update_total) + norm_eps)
    fresh = weight - learn_rate * trust_ratio[:, None, None] * update
    return fresh.astype(jnp.bfloat16)


def solution(mesh):
    placed = (
        P(("expert", "dp"), None),
        P(("expert", "dp"), None, None),
        P(("expert", "dp"), None),
        P(("expert", "dp"), None),
        P(("expert", "dp"), None),
        P("expert", "dp", None),
        P("expert", "dp", None),
        P("expert", "dp", None),
    )
    return jax.shard_map(
        local, mesh=mesh, in_specs=placed, out_specs=P("expert", "dp", None), check_vma=False
    )
```

profile of v0, /device:TPU:0, one launch (start us, length us, event | category | flops | bytes accessed | tf_op | source)
XLA Modules:
  0.0 151.3 jit_solution(233067076570586812)
XLA Ops:
  6.5 0.0 copy-start
  6.5 0.8 reshape.83
  7.4 0.8 reshape.82
  8.2 0.0 copy-done
  8.2 0.0 copy-start.3
  8.2 0.0 copy-start.4
  8.2 0.0 copy-start.2
  8.2 0.7 gather_fusion
  8.9 0.8 broadcast_select_fusion
  9.7 6.3 %all-to-all-start = ((bf16[4,16,2048]{2,1,0:T(8,128)(2,1)}), bf16[4,16,2048]{2,1,0:T(8,128)(2,1)S(1)}, u32[]{:S(2)}, u32[]{:S(2)}) async-start(bf16[4,16,2048]{2,1,0:T(8,128)(2,1)} %broadcast_select_fusion), calls=%async_computation | async-start | bytes 524288 | tf_op jit(solution)/shard_map/all_to_all | solution.py:28
  16.1 0.0 reduce-scatter.9.cloned.1.call-start
  16.1 0.6 broadcast.63
  16.7 0.0 copy-done.3
  16.7 0.7 reduce.6
  17.4 0.1 reshape.81
  17.5 0.6 broadcast.64
  18.1 0.0 copy-done.4
  18.1 0.7 reduce.7
  18.8 0.1 lt.36
  18.9 0.1 fusion.14
  19.0 6.0 %all-to-all-done = bf16[4,16,2048]{2,1,0:T(8,128)(2,1)S(1)} async-done(((bf16[4,16,2048]{2,1,0:T(8,128)(2,1)}), bf16[4,16,2048]{2,1,0:T(8,128)(2,1)S(1)}, u32[]{:S(2)}, u32[]{:S(2)}) %all-to-all-start) | async-done | bytes 262176 | tf_op jit(solution)/shard_map/all_to_all | solution.py:28
  25.0 0.1 fusion.12
  25.1 0.0 copy-done.2
  25.1 2.7 %fusion.1 = bf16[768,2048]{0,1:T(8,128)(2,1)} fusion(bf16[4,2,8,2048]{3,2,0,1:T(8,128)(2,1)S(1)} %fusion.12, bf16[4,2,8,768]{3,2,1,0:T(8,128)(2,1)S(1)} %bitcast.43), kind=kOutput, calls=%fused_computation.4 | convolution fusion | flops 102236160 | bytes 3325952 | tf_op jit(solution)/shard_map/dot_general | solution.py:43
  27.9 4.8 %copy.38 = bf16[768,2048]{1,0:T(8,128)(2,1)} copy(bf16[768,2048]{0,1:T(8,128)(2,1)} %fusion.1) | data formatting | bytes 6291456
  32.6 0.0 reduce-scatter.9.cloned.1.call-update
  32.6 0.0 reduce-scatter.7.cloned.1.call-start
  32.7 2.7 %fusion = bf16[768,2048]{0,1:T(8,128)(2,1)} fusion(bf16[4,2,8,2048]{3,2,0,1:T(8,128)(2,1)S(1)} %fusion.12, bf16[4,2,8,768]{3,2,1,0:T(8,128)(2,1)S(1)} %bitcast.44), kind=kOutput, calls=%fused_computation.3 | convolution fusion | flops 102236160 | bytes 3325952 | tf_op jit(solution)/shard_map/dot_general | solution.py:43
  35.4 4.7 %copy.36 = bf16[768,2048]{1,0:T(8,128)(2,1)} copy(bf16[768,2048]{0,1:T(8,128)(2,1)} %fusion) | data formatting | bytes 6291456
  40.2 0.0 copy-start.1
  40.2 0.0 reduce-scatter.7.cloned.1.call-update
  40.2 37.7 %reduce-scatter.9.cloned.1.call-done = bf16[96,2048]{1,0:T(8,128)(2,1)} async-done(((bf16[768,2048]{1,0:T(8,128)(2,1)}), bf16[96,2048]{1,0:T(8,128)(2,1)}) %reduce-scatter.9.cloned.1.call-update) | async-done | bytes 393232 | tf_op jit(solution)/shard_map/reduce_scatter | solution.py:45
  77.9 49.5 %reduce-scatter.7.cloned.1.call-done = bf16[96,2048]{1,0:T(8,128)(2,1)} async-done(((bf16[768,2048]{1,0:T(8,128)(2,1)}), bf16[96,2048]{1,0:T(8,128)(2,1)}) %reduce-scatter.7.cloned.1.call-update) | async-done | bytes 393232 | tf_op jit(solution)/shard_map/reduce_scatter | solution.py:45
  127.4 0.0 copy-done.1
  127.4 3.4 %multiply_reduce_fusion = (f32[2]{0:T(128)S(1)}, f32[2,96,2048]{2,1,0:T(8,128)S(1)}, f32[2]{0:T(128)S(1)}) fusion(bf16[2,96,2048]{2,1,0:T(8,128)(2,1)S(1)} %copy-done.1, bf16[2,96,2048]{2,1,0:T(8,128)(2,1)} %param.15, bf16[1,96,2048]{2,1,0:T(8,128)(2,1)} %bitcast.41, bf16[1,96,2048]{2,1,0:T(8,128)(2,1)} %bitcast.42, bf16[2,96,2048]{2,1,0:T(8,128)(2,1)} %param.14), kind=kLoop, calls=%fused_computation.20 | loop fusion | flops 8650748 | bytes 4718608 | tf_op jit(solution)/shard_map/reduce_sum | solution.py:58
  130.8 12.5 %all-reduce = (f32[2]{0:T(128)S(1)}, f32[2]{0:T(128)S(1)}) all-reduce(f32[2]{0:T(128)S(1)} %get-tuple-element.7, f32[2]{0:T(128)S(1)} %get-tuple-element.9), channel_id=1, replica_groups=mesh['expert'=4,'dp'=8] {'dp'}, use_global_device_ids=true, to_apply=%region_5.6 | all-reduce | flops 4 | bytes 32 | tf_op jit(solution)/shard_map/psum | solution.py:59
  143.3 1.2 fusion.7
  (5 shorter events, 0.0 us)
Async XLA Ops:
  6.5 1.6 %copy-start = (bf16[128,2048]{1,0:T(8,128)(2,1)S(1)}, bf16[128,2048]{1,0:T(8,128)(2,1)}, u32[]{:S(2)}) copy-start(bf16[128,2048]{1,0:T(8,128)(2,1)} %param.8) | copy-start | bytes 1572868
  8.2 8.5 %copy-start.3 = (f32[1,64]{1,0:T(1,128)S(1)}, f32[1,64]{1,0:T(1,128)}, u32[]{:S(2)}) copy-start(f32[1,64]{1,0:T(1,128)} %param.11) | copy-start | bytes 772
  8.2 9.9 %copy-start.4 = (s32[1,8]{1,0:T(1,128)S(1)}, s32[1,8]{1,0:T(1,128)}, u32[]{:S(2)}) copy-start(s32[1,8]{1,0:T(1,128)} %param.12) | copy-start | bytes 100
  8.2 16.9 %copy-start.2 = (bf16[64,768]{1,0:T(8,128)(2,1)S(1)}, bf16[64,768]{1,0:T(8,128)(2,1)}, u32[]{:S(2)}) copy-start(bf16[64,768]{1,0:T(8,128)(2,1)} %param.10) | copy-start | bytes 294916
  9.7 15.3 %all-to-all-start = ((bf16[4,16,2048]{2,1,0:T(8,128)(2,1)}), bf16[4,16,2048]{2,1,0:T(8,128)(2,1)S(1)}, u32[]{:S(2)}, u32[]{:S(2)}) async-start(bf16[4,16,2048]{2,1,0:T(8,128)(2,1)} %broadcast_select_fusion), calls=%async_computation | async-start | bytes 524288 | tf_op jit(solution)/shard_map/all_to_all | solution.py:28
  16.1 61.8 %reduce-scatter.9.cloned.1.call-start = ((), (), s32[]{:S(2)}) async-start(), calls=%async_computation.4 | async-start | bytes 3538944 | tf_op jit(solution)/shard_map/reduce_scatter | solution.py:45
  32.6 94.7 %reduce-scatter.7.cloned.1.call-start = ((), (), s32[]{:S(2)}) async-start(), calls=%async_computation.3 | async-start | bytes 3538944 | tf_op jit(solution)/shard_map/reduce_scatter | solution.py:45
  40.2 87.2 %copy-start.1 = (bf16[2,96,2048]{2,1,0:T(8,128)(2,1)S(1)}, bf16[2,96,2048]{2,1,0:T(8,128)(2,1)}, u32[]{:S(2)}) copy-start(bf16[2,96,2048]{2,1,0:T(8,128)(2,1)} %param.13) | copy-start | bytes 2359300
Sparse Core Ops, SparseCore 0:
  32.8 45.1 reduce-scatter.8
  81.3 46.0 reduce-scatter.6
where the time goes:
time: 152 us; the launch traced here: 151 us
  waiting for transfers between devices  93.3 us (61%)
  between operations  13.5 us (9%)
  local copies, waits for them, and re-layouts  13.2 us (9%)
  blocking collectives  12.5 us (8%)
  other arithmetic  6.99 us (5%)
  starting transfers between devices  6.39 us (4%)
  matrix products  5.46 us (4%)
    reduce_scatter x2, waiting for transfers between devices, local(): lax.psum_scatter(term.astype(jnp.bfloat16).astype(jnp.float32).astype(jnp...  87.2 us
    psum x1, blocking collectives, local(): update_total = lax.psum(update_sq, 'dp')  12.5 us
    unnamed x14, local copies, waits for them, and re-layouts  10.7 us
    all_to_all x1, starting transfers between devices, local(): lax.all_to_all(picked, 'expert', split_axis=0, concat_axis=0, tiled=True)  6.35 us
    all_to_all x1, waiting for transfers between devices, local(): lax.all_to_all(picked, 'expert', split_axis=0, concat_axis=0, tiled=True)  6.05 us
    dot_general x2, matrix products, local(): jnp.dot(saved_rows.T, scaled_rows, preferred_element_type=jnp.float32)  5.46 us
    reduce_sum x1, other arithmetic, local(): update_sq = jnp.sum(update * update, axis=(1, 2))  3.4 us
  transfers between devices with their start and end apart: 3, of which 3 were waited for; matrix products, arithmetic and copies ran while one was open for 7% of the time, Pallas kernels for 0%

commit v1 on v0

--- a/solution.py
+++ b/solution.py
@@ -56,7 +56,11 @@
         first_new / bias_one / (jnp.sqrt(second_new / bias_two) + adam_eps) + decay_rate * weight
     )
     update_sq = jnp.sum(update * update, axis=(1, 2))
-    update_total = lax.psum(update_sq, "dp")
+    update_total = update_sq
+    for hop in (1, 2, 4):
+        update_total = update_total + lax.ppermute(
+            update_total, "dp", [(dev, dev ^ hop) for dev in range(8)]
+        )
     trust_ratio = jnp.sqrt(weight_total) / (jnp.sqrt(update_total) + norm_eps)
     fresh = weight - learn_rate * trust_ratio[:, None, None] * update
     return fresh.astype(jnp.bfloat16)

time: 152 us -> 160 us (1.053)
  waiting for transfers between devices: 93.3 us -> 100 us
    ppermute x0 -> x3, waiting for transfers between devices: none -> 6.83 us  [local(): lax.ppermute(update_total, 'dp', [(dev, dev ^ hop) for dev in range(8)])]
  transfers between devices with their start and end apart: 3 -> 6, of which waited for: 3 -> 6; matrix products, arithmetic and copies ran while one was open for 7% -> 6% of each run, Pallas kernels for 0% -> 0%
where the time goes in v1:
time: 160 us
  waiting for transfers between devices  100 us (62%)
  between operations  13.5 us (8%)
  local copies, waits for them, and re-layouts  13.2 us (8%)
  blocking collectives  12.5 us (8%)
  starting transfers between devices  7.9 us (5%)
  other arithmetic  6.99 us (4%)
  matrix products  5.46 us (3%)
    reduce_scatter x2, waiting for transfers between devices, local(): lax.psum_scatter(term.astype(jnp.bfloat16).astype(jnp.float32).astype(jnp...  87.2 us
    psum x1, blocking collectives, local(): weight_total = lax.psum(weight_sq, 'dp')  12.5 us
    unnamed x14, local copies, waits for them, and re-layouts  10.7 us
    ppermute x3, waiting for transfers between devices, local(): lax.ppermute(update_total, 'dp', [(dev, dev ^ hop) for dev in range(8)])  6.83 us
    all_to_all x1, starting transfers between devices, local(): lax.all_to_all(picked, 'expert', split_axis=0, concat_axis=0, tiled=True)  6.35 us
    all_to_all x1, waiting for transfers between devices, local(): lax.all_to_all(picked, 'expert', split_axis=0, concat_axis=0, tiled=True)  6.05 us
    dot_general x2, matrix products, local(): jnp.dot(saved_rows.T, scaled_rows, preferred_element_type=jnp.float32)  5.46 us
    reduce_sum x1, other arithmetic, local(): update_sq = jnp.sum(update * update, axis=(1, 2))  3.4 us
  transfers between devices with their start and end apart: 6, of which 6 were waited for; matrix products, arithmetic and copies ran while one was open for 6% of the time, Pallas kernels for 0%

profile of v1, /device:TPU:0, one launch (start us, length us, event | category | flops | bytes accessed | tf_op | source)
XLA Modules:
  0.0 159.7 jit_solution(11186638025631292904)
XLA Ops:
  6.5 0.0 copy-start
  6.5 0.8 reshape.83
  7.4 0.8 reshape.82
  8.2 0.0 copy-done
  8.2 0.0 copy-start.3
  8.2 0.0 copy-start.4
  8.2 0.0 copy-start.2
  8.2 0.7 gather_fusion
  8.9 0.8 broadcast_select_fusion
  9.7 6.3 %all-to-all-start = ((bf16[4,16,2048]{2,1,0:T(8,128)(2,1)}), bf16[4,16,2048]{2,1,0:T(8,128)(2,1)S(1)}, u32[]{:S(2)}, u32[]{:S(2)}) async-start(bf16[4,16,2048]{2,1,0:T(8,128)(2,1)} %broadcast_select_fusion), calls=%async_computation | async-start | bytes 524288 | tf_op jit(solution)/shard_map/all_to_all | solution.py:28
  16.1 0.0 reduce-scatter.9.cloned.1.call-start
  16.1 0.6 broadcast.63
  16.7 0.0 copy-done.3
  16.7 0.7 reduce.6
  17.4 0.1 reshape.81
  17.5 0.6 broadcast.64
  18.1 0.0 copy-done.4
  18.1 0.7 reduce.7
  18.8 0.1 lt.36
  18.9 0.1 fusion.14
  19.0 6.0 %all-to-all-done = bf16[4,16,2048]{2,1,0:T(8,128)(2,1)S(1)} async-done(((bf16[4,16,2048]{2,1,0:T(8,128)(2,1)}), bf16[4,16,2048]{2,1,0:T(8,128)(2,1)S(1)}, u32[]{:S(2)}, u32[]{:S(2)}) %all-to-all-start) | async-done | bytes 262176 | tf_op jit(solution)/shard_map/all_to_all | solution.py:28
  25.0 0.1 fusion.12
  25.1 0.0 copy-done.2
  25.1 2.7 %fusion.1 = bf16[768,2048]{0,1:T(8,128)(2,1)} fusion(bf16[4,2,8,2048]{3,2,0,1:T(8,128)(2,1)S(1)} %fusion.12, bf16[4,2,8,768]{3,2,1,0:T(8,128)(2,1)S(1)} %bitcast.43), kind=kOutput, calls=%fused_computation.4 | convolution fusion | flops 102236160 | bytes 3325952 | tf_op jit(solution)/shard_map/dot_general | solution.py:43
  27.9 4.8 %copy.38 = bf16[768,2048]{1,0:T(8,128)(2,1)} copy(bf16[768,2048]{0,1:T(8,128)(2,1)} %fusion.1) | data formatting | bytes 6291456
  32.6 0.0 reduce-scatter.9.cloned.1.call-update
  32.6 0.0 reduce-scatter.7.cloned.1.call-start
  32.7 2.7 %fusion = bf16[768,2048]{0,1:T(8,128)(2,1)} fusion(bf16[4,2,8,2048]{3,2,0,1:T(8,128)(2,1)S(1)} %fusion.12, bf16[4,2,8,768]{3,2,1,0:T(8,128)(2,1)S(1)} %bitcast.44), kind=kOutput, calls=%fused_computation.3 | convolution fusion | flops 102236160 | bytes 3325952 | tf_op jit(solution)/shard_map/dot_general | solution.py:43
  35.4 4.7 %copy.36 = bf16[768,2048]{1,0:T(8,128)(2,1)} copy(bf16[768,2048]{0,1:T(8,128)(2,1)} %fusion) | data formatting | bytes 6291456
  40.2 0.0 copy-start.1
  40.2 0.0 reduce-scatter.7.cloned.1.call-update
  40.2 37.7 %reduce-scatter.9.cloned.1.call-done = bf16[96,2048]{1,0:T(8,128)(2,1)} async-done(((bf16[768,2048]{1,0:T(8,128)(2,1)}), bf16[96,2048]{1,0:T(8,128)(2,1)}) %reduce-scatter.9.cloned.1.call-update) | async-done | bytes 393232 | tf_op jit(solution)/shard_map/reduce_scatter | solution.py:45
  77.9 49.5 %reduce-scatter.7.cloned.1.call-done = bf16[96,2048]{1,0:T(8,128)(2,1)} async-done(((bf16[768,2048]{1,0:T(8,128)(2,1)}), bf16[96,2048]{1,0:T(8,128)(2,1)}) %reduce-scatter.7.cloned.1.call-update) | async-done | bytes 393232 | tf_op jit(solution)/shard_map/reduce_scatter | solution.py:45
  127.4 0.0 copy-done.1
  127.4 3.4 %multiply_reduce_fusion = (f32[2]{0:T(128)S(1)}, f32[2,96,2048]{2,1,0:T(8,128)S(1)}, f32[2]{0:T(128)S(1)}) fusion(bf16[2,96,2048]{2,1,0:T(8,128)(2,1)S(1)} %copy-done.1, bf16[2,96,2048]{2,1,0:T(8,128)(2,1)} %param.15, bf16[1,96,2048]{2,1,0:T(8,128)(2,1)} %bitcast.41, bf16[1,96,2048]{2,1,0:T(8,128)(2,1)} %bitcast.42, bf16[2,96,2048]{2,1,0:T(8,128)(2,1)} %param.14), kind=kLoop, calls=%fused_computation.20 | loop fusion | flops 8650748 | bytes 4718608 | tf_op jit(solution)/shard_map/reduce_sum | solution.py:58
  130.8 12.5 %psum.7 = f32[2]{0:T(128)S(1)} all-reduce(f32[2]{0:T(128)S(1)} %get-tuple-element.7), channel_id=1, replica_groups=mesh['expert'=4,'dp'=8] {'dp'}, use_global_device_ids=true, to_apply=%region_1.0 | all-reduce | flops 2 | bytes 16 | tf_op jit(solution)/shard_map/psum | solution.py:24
  143.3 0.1 collective-permute-start
  143.4 1.1 collective-permute-done
  144.5 0.0 collective-permute-start.1
  144.5 3.6 %collective-permute-done.1 = f32[2]{0:T(128)S(1)} collective-permute-done((f32[2]{0:T(128)S(1)}, f32[2]{0:T(128)S(1)}, u32[]{:S(2)}, u32[]{:S(2)}) %collective-permute-start.1) | collective-permute-done | bytes 40 | tf_op jit(solution)/shard_map/ppermute | solution.py:61
  148.1 1.4 collective-permute-start.2
  149.5 2.1 %collective-permute-done.2 = f32[2]{0:T(128)S(1)} collective-permute-done((f32[2]{0:T(128)S(1)}, f32[2]{0:T(128)S(1)}, u32[]{:S(2)}, u32[]{:S(2)}) %collective-permute-start.2) | collective-permute-done | bytes 40 | tf_op jit(solution)/shard_map/ppermute | solution.py:61
  151.7 1.2 fusion.7
  (7 shorter events, 0.0 us)
Async XLA Ops:
  6.5 1.6 %copy-start = (bf16[128,2048]{1,0:T(8,128)(2,1)S(1)}, bf16[128,2048]{1,0:T(8,128)(2,1)}, u32[]{:S(2)}) copy-start(bf16[128,2048]{1,0:T(8,128)(2,1)} %param.8) | copy-start | bytes 1572868
  8.2 8.5 %copy-start.3 = (f32[1,64]{1,0:T(1,128)S(1)}, f32[1,64]{1,0:T(1,128)}, u32[]{:S(2)}) copy-start(f32[1,64]{1,0:T(1,128)} %param.11) | copy-start | bytes 772
  8.2 9.9 %copy-start.4 = (s32[1,8]{1,0:T(1,128)S(1)}, s32[1,8]{1,0:T(1,128)}, u32[]{:S(2)}) copy-start(s32[1,8]{1,0:T(1,128)} %param.12) | copy-start | bytes 100
  8.2 16.9 %copy-start.2 = (bf16[64,768]{1,0:T(8,128)(2,1)S(1)}, bf16[64,768]{1,0:T(8,128)(2,1)}, u32[]{:S(2)}) copy-start(bf16[64,768]{1,0:T(8,128)(2,1)} %param.10) | copy-start | bytes 294916
  9.7 15.3 %all-to-all-start = ((bf16[4,16,2048]{2,1,0:T(8,128)(2,1)}), bf16[4,16,2048]{2,1,0:T(8,128)(2,1)S(1)}, u32[]{:S(2)}, u32[]{:S(2)}) async-start(bf16[4,16,2048]{2,1,0:T(8,128)(2,1)} %broadcast_select_fusion), calls=%async_computation | async-start | bytes 524288 | tf_op jit(solution)/shard_map/all_to_all | solution.py:28
  16.1 61.8 %reduce-scatter.9.cloned.1.call-start = ((), (), s32[]{:S(2)}) async-start(), calls=%async_computation.4 | async-start | bytes 3538944 | tf_op jit(solution)/shard_map/reduce_scatter | solution.py:45
  32.6 94.7 %reduce-scatter.7.cloned.1.call-start = ((), (), s32[]{:S(2)}) async-start(), calls=%async_computation.3 | async-start | bytes 3538944 | tf_op jit(solution)/shard_map/reduce_scatter | solution.py:45
  40.2 87.2 %copy-start.1 = (bf16[2,96,2048]{2,1,0:T(8,128)(2,1)S(1)}, bf16[2,96,2048]{2,1,0:T(8,128)(2,1)}, u32[]{:S(2)}) copy-start(bf16[2,96,2048]{2,1,0:T(8,128)(2,1)} %param.13) | copy-start | bytes 2359300
  143.3 1.2 collective-permute-start
  144.5 3.6 %collective-permute-start.1 = (f32[2]{0:T(128)S(1)}, f32[2]{0:T(128)S(1)}, u32[]{:S(2)}, u32[]{:S(2)}) collective-permute-start(f32[2]{0:T(128)S(1)} %add.64), channel_id=1, source_target_pairs={{0,2},{1,3},{2,0},{3,1},{4,6},{5,7},{6,4},{7,5},{8,10},{9,11},{10,... | collective-permute-start | bytes 32 | tf_op jit(solution)/shard_map/ppermute | solution.py:61
  148.1 3.6 %collective-permute-start.2 = (f32[2]{0:T(128)S(1)}, f32[2]{0:T(128)S(1)}, u32[]{:S(2)}, u32[]{:S(2)}) collective-permute-start(f32[2]{0:T(128)S(1)} %add.65), channel_id=1, source_target_pairs={{0,4},{1,5},{2,6},{3,7},{4,0},{5,1},{6,2},{7,3},{8,12},{9,13},{10,... | collective-permute-start | bytes 32 | tf_op jit(solution)/shard_map/ppermute | solution.py:61
Sparse Core Ops, SparseCore 0:
  32.8 45.1 reduce-scatter.8
  81.3 46.0 reduce-scatter.6
